TPU v7x, 256 devices: a whole 4x4x8 slice. The times are simulated.
256 devices in a mesh: tile: 64 (over y, z, core), sec: 4 (over x).
Axes of the slice: x: 4, y: 4, z: 8, core: 2. Of those that a mesh axis runs over, the one named last changes fastest.
Arguments:
- voltage: float32 [8192, 512], P('tile', 'sec'), may hold values from -6 to 6
- conductance: float32 [8192, 512], P('tile', 'sec'), may hold values from 0.2 to 2
- reversal: float32 [8192, 512], P('tile', 'sec'), may hold values from -1 to 1
- drive: bfloat16 [8, 8192, 512], P(None, 'tile', 'sec'), may hold values from -6 to 6
- inv_cable: float32 [128, 128], replicated, may hold values from -1 to 1
- owner_map: int32 [8192], P('tile'), may hold values from 0 to 63, as said below
- peer_counts: int32 [64, 64], P('tile'), may hold values from 0 to 4, as said below
- pattern: int32 [4, 8192, 2], P('sec', 'tile'), may hold values from 0 to 31, all different within a row
- transfer: bfloat16 [4, 8192, 2, 128, 128], P('sec', 'tile'), may hold values from -0.01171875 to 0.01171875
Outputs:
- final_voltage: float32 [8192, 512], P('tile', 'sec')
- probe: float32 [8, 4096], P(None, ('tile', 'sec'))
Inputs may be any that keep to these rules, and one draw needn't show every extreme that they name: `owner_map`: every depth tile owns exactly 128 cells; the cells c with c // 128 = u include at most 4 cells of one owner, and exactly 4 of some owner. peer_counts[d, u] is the number of cells c with c // 128 = u and owner_map[c] = d. `pattern`: the 2 contact tiles of one slot and section differ.
All inputs are finite; a program needn't handle non-finite values.
Results may differ from a plain program's by a relative error of at most 0.0029.
Values may be sent and summed in bfloat16 or wider, within the bound.
A program may use at most 64 MiB of HBM per device.

v0:
```python
import jax
import jax.numpy as jnp
from jax import lax
from jax.sharding import PartitionSpec as P

CONTACTS = 4096
TIME_STEP = 0.25
AXIAL = 2.0


def padded_2(block, sides, width):
    for axis, dim in sides:
        count = lax.axis_size(axis)
        forward = [(i, i + 1) for i in range(count - 1)]
        backward = [(target, source) for source, target in forward]
        low = lax.ppermute(
            lax.slice_in_dim(block, block.shape[dim] - width, None, axis=dim), axis, forward
        )
        high = lax.ppermute(lax.slice_in_dim(block, 0, width, axis=dim), axis, backward)
        block = jnp.concatenate([low, block, high], axis=dim)
    return block


def cable_update(voltage_now, conductance, reversal, drive_now, inv_cable):
    padded = padded_2(voltage_now.astype(jnp.bfloat16), (("sec", 1),), 1).astype(voltage_now.dtype)
    columns = jnp.arange(voltage_now.shape[1], dtype=jnp.int32)
    first_col = (columns == 0).astype(jnp.float32)
    last_col = (columns == voltage_now.shape[1] - 1).astype(jnp.float32)
    boundary = first_col * (padded[:, :-2] - voltage_now) + last_col * (padded[:, 2:] - voltage_now)
    driven = drive_now.astype(jnp.float32)
    right_side = voltage_now * (1.0 - TIME_STEP * conductance) + TIME_STEP * (
        conductance * reversal + driven + AXIAL * boundary
    )
    voltage_next = jnp.einsum("ci,ji->cj", right_side, inv_cable, precision=lax.Precision.HIGHEST)
    current = (conductance * (voltage_next - reversal) - driven).astype(jnp.bfloat16)
    return (voltage_next, current)


def on_device(
    voltage, conductance, reversal, drive, inv_cable, owner_map, peer_counts, pattern, transfer
):
    cell_count = voltage.shape[0]
    seg_width = voltage.shape[1]
    step_count = drive.shape[0]
    tile_count = lax.axis_size("tile")
    section_count = lax.axis_size("sec")
    capacity = 2 * cell_count // tile_count
    owners = jnp.arange(tile_count, dtype=jnp.int32)
    member = (owner_map[:, None] == owners[None, :]).astype(jnp.int32)
    rank_within = jnp.sum(jnp.cumsum(member, axis=0) * member, axis=1) - 1
    placed = owner_map * capacity + rank_within
    source_row = (
        jnp.full((tile_count * capacity,), cell_count, jnp.int32)
        .at[placed]
        .set(jnp.arange(cell_count, dtype=jnp.int32))
    )
    blank_row = jnp.zeros((1, seg_width), jnp.bfloat16)

    def advance_send(voltage_now, drive_now):
        voltage_next, current = cable_update(
            voltage_now, conductance, reversal, drive_now, inv_cable
        )
        outgoing = jnp.take(jnp.concatenate([current, blank_row], axis=0), source_row, axis=0)
        outgoing = outgoing.reshape(tile_count, capacity, seg_width)
        arrived = lax.all_to_all(outgoing, "tile", split_axis=0, concat_axis=0, tiled=True)
        return (voltage_next, arrived)

    final_voltage, arrived = lax.scan(advance_send, voltage, drive)
    received = arrived.reshape(step_count, tile_count * capacity, seg_width)
    counts = peer_counts[0]
    end_rows = jnp.cumsum(counts)
    starts = end_rows - counts
    slot_ids = jnp.arange(cell_count, dtype=jnp.int32)
    source = jnp.sum((end_rows[None, :] <= slot_ids[:, None]).astype(jnp.int32), axis=1)
    offset = jnp.sum(jnp.where(source[:, None] == owners[None, :], starts[None, :], 0), axis=1)
    gather_rows = source * capacity + slot_ids - offset
    ordered = jnp.take(received, gather_rows, axis=1)
    weights = transfer[0]
    layout = pattern[0]
    contact_width = weights.shape[3]
    tile_total = CONTACTS // contact_width
    tile_sums = jnp.einsum("tsi,skic->tskc", ordered, weights, preferred_element_type=jnp.float32)
    select = (layout[:, :, None] == jnp.arange(tile_total, dtype=jnp.int32)[None, None, :]).astype(
        jnp.float32
    )
    partial_sum = jnp.einsum("tskc,skq->tqc", tile_sums, select, precision=lax.Precision.HIGHEST)
    partial_sum = partial_sum.reshape(step_count, tile_total * contact_width)
    summed = lax.psum(partial_sum, ("tile", "sec"))
    share_width = summed.shape[1] // (tile_count * section_count)
    position = lax.axis_index("tile") * section_count + lax.axis_index("sec")
    probe_share = lax.dynamic_slice_in_dim(summed, position * share_width, share_width, 1)
    return (final_voltage, probe_share)


def solution(mesh):
    placed = (
        P("tile", "sec"),
        P("tile", "sec"),
        P("tile", "sec"),
        P(None, "tile", "sec"),
        P(),
        P("tile"),
        P("tile", None),
        P("sec", "tile", None),
        P("sec", "tile", None, None, None),
    )
    return jax.shard_map(
        on_device,
        mesh=mesh,
        in_specs=placed,
        out_specs=(P("tile", "sec"), P(None, ("tile", "sec"))),
        check_vma=False,
    )
```

profile of v0, /device:TPU:8, one launch (start us, length us, event | category | flops | bytes accessed | tf_op | source)
XLA Modules:
  0.0 478.0 jit_solution(9085325909894427495)
XLA Ops:
  14.3 208.3 %while.13 = (s32[]{:T(128)}, f32[128,128]{1,0:T(8,128)S(1)}, bf16[8,64,4,128]{3,2,1,0:T(4,128)(2,1)S(1)}, f32[128,128]{1,0:T(8,128)}, bf16[8,128,128]{2,1,0:T(8,...) while((s32[]{:T(128)}, f32[128,128]{1,0:T(8,128)S(1)}, ...), condition=%wide.region_4.5_spmd, body=%wide.region_3.4_spmd.sunk | while | flops 25629952 | bytes 1626603 | solution.py:68
  15.7 4.5 collective-permute-start.1
  20.4 1.4 collective-permute-done.1
  24.8 12.1 %all-to-all-start = ((bf16[64,4,128]{2,1,0:T(4,128)(2,1)}), bf16[64,4,128]{2,1,0:T(4,128)(2,1)S(1)}, u32[]{:S(2)}, u32[]{:S(2)}) async-start(bf16[64,4,128]{2,1,0:T(4,128)(2,1)} %broadcast_select_fusion.2), calls=%async_computation | async-start | bytes 131072 | tf_op jit(solution)/shard_map/while/body/eval_jaxpr/all_to_all | solution.py:65
  36.9 8.8 %all-to-all-done = bf16[64,4,128]{2,1,0:T(4,128)(2,1)S(1)} async-done(((bf16[64,4,128]{2,1,0:T(4,128)(2,1)}), bf16[64,4,128]{2,1,0:T(4,128)(2,1)S(1)}, u32[]{:S(2)}, u32[]{:S(2)}) %all-to-all-start) | async-done | bytes 65568 | tf_op jit(solution)/shard_map/while/body/eval_jaxpr/all_to_all | solution.py:65
  47.2 4.9 %collective-permute-start.1 = (bf16[128,1]{1,0:T(8,128)(2,1)S(1)}, bf16[128,1]{1,0:T(8,128)(2,1)S(1)}, u32[]{:S(2)}, u32[]{:S(2)}) collective-permute-start(bf16[128,1]{1,0:T(8,128)(2,1)S(1)} %get-tuple-element.171), channel_id=1, source_target_pairs={{0,1},{1,2},{2,3},{4,5},{5,6},{6,7},{8,9},{9,10},{10,11},{12,13},{... | collective-permute-start | bytes 776 | tf_op jit(solution)/shard_map/while/body/eval_jaxpr/ppermute | solution.py:16
  52.2 1.4 collective-permute-done.1
  56.7 5.5 %all-to-all-start = ((bf16[64,4,128]{2,1,0:T(4,128)(2,1)}), bf16[64,4,128]{2,1,0:T(4,128)(2,1)S(1)}, u32[]{:S(2)}, u32[]{:S(2)}) async-start(bf16[64,4,128]{2,1,0:T(4,128)(2,1)} %broadcast_select_fusion.2), calls=%async_computation | async-start | bytes 131072 | tf_op jit(solution)/shard_map/while/body/eval_jaxpr/all_to_all | solution.py:65
  62.2 8.8 %all-to-all-done = bf16[64,4,128]{2,1,0:T(4,128)(2,1)S(1)} async-done(((bf16[64,4,128]{2,1,0:T(4,128)(2,1)}), bf16[64,4,128]{2,1,0:T(4,128)(2,1)S(1)}, u32[]{:S(2)}, u32[]{:S(2)}) %all-to-all-start) | async-done | bytes 65568 | tf_op jit(solution)/shard_map/while/body/eval_jaxpr/all_to_all | solution.py:65
  72.5 4.9 %collective-permute-start.1 = (bf16[128,1]{1,0:T(8,128)(2,1)S(1)}, bf16[128,1]{1,0:T(8,128)(2,1)S(1)}, u32[]{:S(2)}, u32[]{:S(2)}) collective-permute-start(bf16[128,1]{1,0:T(8,128)(2,1)S(1)} %get-tuple-element.171), channel_id=1, source_target_pairs={{0,1},{1,2},{2,3},{4,5},{5,6},{6,7},{8,9},{9,10},{10,11},{12,13},{... | collective-permute-start | bytes 776 | tf_op jit(solution)/shard_map/while/body/eval_jaxpr/ppermute | solution.py:16
  77.5 1.4 collective-permute-done.1
  81.9 5.5 %all-to-all-start = ((bf16[64,4,128]{2,1,0:T(4,128)(2,1)}), bf16[64,4,128]{2,1,0:T(4,128)(2,1)S(1)}, u32[]{:S(2)}, u32[]{:S(2)}) async-start(bf16[64,4,128]{2,1,0:T(4,128)(2,1)} %broadcast_select_fusion.2), calls=%async_computation | async-start | bytes 131072 | tf_op jit(solution)/shard_map/while/body/eval_jaxpr/all_to_all | solution.py:65
  87.4 8.8 %all-to-all-done = bf16[64,4,128]{2,1,0:T(4,128)(2,1)S(1)} async-done(((bf16[64,4,128]{2,1,0:T(4,128)(2,1)}), bf16[64,4,128]{2,1,0:T(4,128)(2,1)S(1)}, u32[]{:S(2)}, u32[]{:S(2)}) %all-to-all-start) | async-done | bytes 65568 | tf_op jit(solution)/shard_map/while/body/eval_jaxpr/all_to_all | solution.py:65
  97.7 4.9 %collective-permute-start.1 = (bf16[128,1]{1,0:T(8,128)(2,1)S(1)}, bf16[128,1]{1,0:T(8,128)(2,1)S(1)}, u32[]{:S(2)}, u32[]{:S(2)}) collective-permute-start(bf16[128,1]{1,0:T(8,128)(2,1)S(1)} %get-tuple-element.171), channel_id=1, source_target_pairs={{0,1},{1,2},{2,3},{4,5},{5,6},{6,7},{8,9},{9,10},{10,11},{12,13},{... | collective-permute-start | bytes 776 | tf_op jit(solution)/shard_map/while/body/eval_jaxpr/ppermute | solution.py:16
  102.8 1.4 collective-permute-done.1
  107.2 5.5 %all-to-all-start = ((bf16[64,4,128]{2,1,0:T(4,128)(2,1)}), bf16[64,4,128]{2,1,0:T(4,128)(2,1)S(1)}, u32[]{:S(2)}, u32[]{:S(2)}) async-start(bf16[64,4,128]{2,1,0:T(4,128)(2,1)} %broadcast_select_fusion.2), calls=%async_computation | async-start | bytes 131072 | tf_op jit(solution)/shard_map/while/body/eval_jaxpr/all_to_all | solution.py:65
  112.7 8.8 %all-to-all-done = bf16[64,4,128]{2,1,0:T(4,128)(2,1)S(1)} async-done(((bf16[64,4,128]{2,1,0:T(4,128)(2,1)}), bf16[64,4,128]{2,1,0:T(4,128)(2,1)S(1)}, u32[]{:S(2)}, u32[]{:S(2)}) %all-to-all-start) | async-done | bytes 65568 | tf_op jit(solution)/shard_map/while/body/eval_jaxpr/all_to_all | solution.py:65
  123.0 4.9 %collective-permute-start.1 = (bf16[128,1]{1,0:T(8,128)(2,1)S(1)}, bf16[128,1]{1,0:T(8,128)(2,1)S(1)}, u32[]{:S(2)}, u32[]{:S(2)}) collective-permute-start(bf16[128,1]{1,0:T(8,128)(2,1)S(1)} %get-tuple-element.171), channel_id=1, source_target_pairs={{0,1},{1,2},{2,3},{4,5},{5,6},{6,7},{8,9},{9,10},{10,11},{12,13},{... | collective-permute-start | bytes 776 | tf_op jit(solution)/shard_map/while/body/eval_jaxpr/ppermute | solution.py:16
  128.0 1.4 collective-permute-done.1
  132.4 5.5 %all-to-all-start = ((bf16[64,4,128]{2,1,0:T(4,128)(2,1)}), bf16[64,4,128]{2,1,0:T(4,128)(2,1)S(1)}, u32[]{:S(2)}, u32[]{:S(2)}) async-start(bf16[64,4,128]{2,1,0:T(4,128)(2,1)} %broadcast_select_fusion.2), calls=%async_computation | async-start | bytes 131072 | tf_op jit(solution)/shard_map/while/body/eval_jaxpr/all_to_all | solution.py:65
  137.9 8.8 %all-to-all-done = bf16[64,4,128]{2,1,0:T(4,128)(2,1)S(1)} async-done(((bf16[64,4,128]{2,1,0:T(4,128)(2,1)}), bf16[64,4,128]{2,1,0:T(4,128)(2,1)S(1)}, u32[]{:S(2)}, u32[]{:S(2)}) %all-to-all-start) | async-done | bytes 65568 | tf_op jit(solution)/shard_map/while/body/eval_jaxpr/all_to_all | solution.py:65
  148.2 4.9 %collective-permute-start.1 = (bf16[128,1]{1,0:T(8,128)(2,1)S(1)}, bf16[128,1]{1,0:T(8,128)(2,1)S(1)}, u32[]{:S(2)}, u32[]{:S(2)}) collective-permute-start(bf16[128,1]{1,0:T(8,128)(2,1)S(1)} %get-tuple-element.171), channel_id=1, source_target_pairs={{0,1},{1,2},{2,3},{4,5},{5,6},{6,7},{8,9},{9,10},{10,11},{12,13},{... | collective-permute-start | bytes 776 | tf_op jit(solution)/shard_map/while/body/eval_jaxpr/ppermute | solution.py:16
  157.7 5.5 %all-to-all-start = ((bf16[64,4,128]{2,1,0:T(4,128)(2,1)}), bf16[64,4,128]{2,1,0:T(4,128)(2,1)S(1)}, u32[]{:S(2)}, u32[]{:S(2)}) async-start(bf16[64,4,128]{2,1,0:T(4,128)(2,1)} %broadcast_select_fusion.2), calls=%async_computation | async-start | bytes 131072 | tf_op jit(solution)/shard_map/while/body/eval_jaxpr/all_to_all | solution.py:65
  163.2 8.8 %all-to-all-done = bf16[64,4,128]{2,1,0:T(4,128)(2,1)S(1)} async-done(((bf16[64,4,128]{2,1,0:T(4,128)(2,1)}), bf16[64,4,128]{2,1,0:T(4,128)(2,1)S(1)}, u32[]{:S(2)}, u32[]{:S(2)}) %all-to-all-start) | async-done | bytes 65568 | tf_op jit(solution)/shard_map/while/body/eval_jaxpr/all_to_all | solution.py:65
  173.5 4.9 %collective-permute-start.1 = (bf16[128,1]{1,0:T(8,128)(2,1)S(1)}, bf16[128,1]{1,0:T(8,128)(2,1)S(1)}, u32[]{:S(2)}, u32[]{:S(2)}) collective-permute-start(bf16[128,1]{1,0:T(8,128)(2,1)S(1)} %get-tuple-element.171), channel_id=1, source_target_pairs={{0,1},{1,2},{2,3},{4,5},{5,6},{6,7},{8,9},{9,10},{10,11},{12,13},{... | collective-permute-start | bytes 776 | tf_op jit(solution)/shard_map/while/body/eval_jaxpr/ppermute | solution.py:16
  182.9 5.5 %all-to-all-start = ((bf16[64,4,128]{2,1,0:T(4,128)(2,1)}), bf16[64,4,128]{2,1,0:T(4,128)(2,1)S(1)}, u32[]{:S(2)}, u32[]{:S(2)}) async-start(bf16[64,4,128]{2,1,0:T(4,128)(2,1)} %broadcast_select_fusion.2), calls=%async_computation | async-start | bytes 131072 | tf_op jit(solution)/shard_map/while/body/eval_jaxpr/all_to_all | solution.py:65
  188.5 8.8 %all-to-all-done = bf16[64,4,128]{2,1,0:T(4,128)(2,1)S(1)} async-done(((bf16[64,4,128]{2,1,0:T(4,128)(2,1)}), bf16[64,4,128]{2,1,0:T(4,128)(2,1)S(1)}, u32[]{:S(2)}, u32[]{:S(2)}) %all-to-all-start) | async-done | bytes 65568 | tf_op jit(solution)/shard_map/while/body/eval_jaxpr/all_to_all | solution.py:65
  198.7 4.9 %collective-permute-start.1 = (bf16[128,1]{1,0:T(8,128)(2,1)S(1)}, bf16[128,1]{1,0:T(8,128)(2,1)S(1)}, u32[]{:S(2)}, u32[]{:S(2)}) collective-permute-start(bf16[128,1]{1,0:T(8,128)(2,1)S(1)} %get-tuple-element.171), channel_id=1, source_target_pairs={{0,1},{1,2},{2,3},{4,5},{5,6},{6,7},{8,9},{9,10},{10,11},{12,13},{... | collective-permute-start | bytes 776 | tf_op jit(solution)/shard_map/while/body/eval_jaxpr/ppermute | solution.py:16
  208.2 5.5 %all-to-all-start = ((bf16[64,4,128]{2,1,0:T(4,128)(2,1)}), bf16[64,4,128]{2,1,0:T(4,128)(2,1)S(1)}, u32[]{:S(2)}, u32[]{:S(2)}) async-start(bf16[64,4,128]{2,1,0:T(4,128)(2,1)} %broadcast_select_fusion.2), calls=%async_computation | async-start | bytes 131072 | tf_op jit(solution)/shard_map/while/body/eval_jaxpr/all_to_all | solution.py:65
  213.7 8.8 %all-to-all-done = bf16[64,4,128]{2,1,0:T(4,128)(2,1)S(1)} async-done(((bf16[64,4,128]{2,1,0:T(4,128)(2,1)}), bf16[64,4,128]{2,1,0:T(4,128)(2,1)S(1)}, u32[]{:S(2)}, u32[]{:S(2)}) %all-to-all-start) | async-done | bytes 65568 | tf_op jit(solution)/shard_map/while/body/eval_jaxpr/all_to_all | solution.py:65
  223.9 4.6 fusion.28
  230.1 239.7 %all-reduce.3.cloned.1.call-done = f32[8,4096]{1,0:T(8,128)} async-done(((f32[8,4096]{1,0:T(8,128)}), f32[8,4096]{1,0:T(8,128)}) %all-reduce.3.cloned.1.call-update) | async-done | bytes 131088 | tf_op jit(solution)/shard_map/psum | solution.py:88
  (160 shorter events, 51.8 us)
Async XLA Ops:
  7.2 462.6 %all-reduce.3.cloned.1.call-start = ((), (), s32[]{:S(2)}) async-start(), calls=%async_computation.1 | async-start | bytes 262144 | tf_op jit(solution)/shard_map/psum | solution.py:88
  14.4 6.0 %collective-permute-start = (bf16[128,1]{1,0:T(8,128)(2,1)S(1)}, bf16[128,1]{1,0:T(8,128)(2,1)S(1)}, u32[]{:S(2)}, u32[]{:S(2)}) collective-permute-start(bf16[128,1]{1,0:T(8,128)(2,1)S(1)} %get-tuple-element.170), channel_id=1, source_target_pairs={{1,0},{2,1},{3,2},{5,4},{6,5},{7,6},{9,8},{10,9},{11,10},{13,12},{... | collective-permute-start | bytes 776 | tf_op jit(solution)/shard_map/while/body/eval_jaxpr/ppermute | solution.py:19
  15.7 6.1 %collective-permute-start.1 = (bf16[128,1]{1,0:T(8,128)(2,1)S(1)}, bf16[128,1]{1,0:T(8,128)(2,1)S(1)}, u32[]{:S(2)}, u32[]{:S(2)}) collective-permute-start(bf16[128,1]{1,0:T(8,128)(2,1)S(1)} %get-tuple-element.171), channel_id=1, source_target_pairs={{0,1},{1,2},{2,3},{4,5},{5,6},{6,7},{8,9},{9,10},{10,11},{12,13},{... | collective-permute-start | bytes 776 | tf_op jit(solution)/shard_map/while/body/eval_jaxpr/ppermute | solution.py:16
  24.8 20.9 %all-to-all-start = ((bf16[64,4,128]{2,1,0:T(4,128)(2,1)}), bf16[64,4,128]{2,1,0:T(4,128)(2,1)S(1)}, u32[]{:S(2)}, u32[]{:S(2)}) async-start(bf16[64,4,128]{2,1,0:T(4,128)(2,1)} %broadcast_select_fusion.2), calls=%async_computation | async-start | bytes 131072 | tf_op jit(solution)/shard_map/while/body/eval_jaxpr/all_to_all | solution.py:65
  45.9 6.3 %collective-permute-start = (bf16[128,1]{1,0:T(8,128)(2,1)S(1)}, bf16[128,1]{1,0:T(8,128)(2,1)S(1)}, u32[]{:S(2)}, u32[]{:S(2)}) collective-permute-start(bf16[128,1]{1,0:T(8,128)(2,1)S(1)} %get-tuple-element.170), channel_id=1, source_target_pairs={{1,0},{2,1},{3,2},{5,4},{6,5},{7,6},{9,8},{10,9},{11,10},{13,12},{... | collective-permute-start | bytes 776 | tf_op jit(solution)/shard_map/while/body/eval_jaxpr/ppermute | solution.py:19
  47.2 6.4 %collective-permute-start.1 = (bf16[128,1]{1,0:T(8,128)(2,1)S(1)}, bf16[128,1]{1,0:T(8,128)(2,1)S(1)}, u32[]{:S(2)}, u32[]{:S(2)}) collective-permute-start(bf16[128,1]{1,0:T(8,128)(2,1)S(1)} %get-tuple-element.171), channel_id=1, source_target_pairs={{0,1},{1,2},{2,3},{4,5},{5,6},{6,7},{8,9},{9,10},{10,11},{12,13},{... | collective-permute-start | bytes 776 | tf_op jit(solution)/shard_map/while/body/eval_jaxpr/ppermute | solution.py:16
  56.7 14.4 %all-to-all-start = ((bf16[64,4,128]{2,1,0:T(4,128)(2,1)}), bf16[64,4,128]{2,1,0:T(4,128)(2,1)S(1)}, u32[]{:S(2)}, u32[]{:S(2)}) async-start(bf16[64,4,128]{2,1,0:T(4,128)(2,1)} %broadcast_select_fusion.2), calls=%async_computation | async-start | bytes 131072 | tf_op jit(solution)/shard_map/while/body/eval_jaxpr/all_to_all | solution.py:65
  71.2 6.3 %collective-permute-start = (bf16[128,1]{1,0:T(8,128)(2,1)S(1)}, bf16[128,1]{1,0:T(8,128)(2,1)S(1)}, u32[]{:S(2)}, u32[]{:S(2)}) collective-permute-start(bf16[128,1]{1,0:T(8,128)(2,1)S(1)} %get-tuple-element.170), channel_id=1, source_target_pairs={{1,0},{2,1},{3,2},{5,4},{6,5},{7,6},{9,8},{10,9},{11,10},{13,12},{... | collective-permute-start | bytes 776 | tf_op jit(solution)/shard_map/while/body/eval_jaxpr/ppermute | solution.py:19
  72.5 6.4 %collective-permute-start.1 = (bf16[128,1]{1,0:T(8,128)(2,1)S(1)}, bf16[128,1]{1,0:T(8,128)(2,1)S(1)}, u32[]{:S(2)}, u32[]{:S(2)}) collective-permute-start(bf16[128,1]{1,0:T(8,128)(2,1)S(1)} %get-tuple-element.171), channel_id=1, source_target_pairs={{0,1},{1,2},{2,3},{4,5},{5,6},{6,7},{8,9},{9,10},{10,11},{12,13},{... | collective-permute-start | bytes 776 | tf_op jit(solution)/shard_map/while/body/eval_jaxpr/ppermute | solution.py:16
  81.9 14.4 %all-to-all-start = ((bf16[64,4,128]{2,1,0:T(4,128)(2,1)}), bf16[64,4,128]{2,1,0:T(4,128)(2,1)S(1)}, u32[]{:S(2)}, u32[]{:S(2)}) async-start(bf16[64,4,128]{2,1,0:T(4,128)(2,1)} %broadcast_select_fusion.2), calls=%async_computation | async-start | bytes 131072 | tf_op jit(solution)/shard_map/while/body/eval_jaxpr/all_to_all | solution.py:65
  96.4 6.3 %collective-permute-start = (bf16[128,1]{1,0:T(8,128)(2,1)S(1)}, bf16[128,1]{1,0:T(8,128)(2,1)S(1)}, u32[]{:S(2)}, u32[]{:S(2)}) collective-permute-start(bf16[128,1]{1,0:T(8,128)(2,1)S(1)} %get-tuple-element.170), channel_id=1, source_target_pairs={{1,0},{2,1},{3,2},{5,4},{6,5},{7,6},{9,8},{10,9},{11,10},{13,12},{... | collective-permute-start | bytes 776 | tf_op jit(solution)/shard_map/while/body/eval_jaxpr/ppermute | solution.py:19
  97.7 6.4 %collective-permute-start.1 = (bf16[128,1]{1,0:T(8,128)(2,1)S(1)}, bf16[128,1]{1,0:T(8,128)(2,1)S(1)}, u32[]{:S(2)}, u32[]{:S(2)}) collective-permute-start(bf16[128,1]{1,0:T(8,128)(2,1)S(1)} %get-tuple-element.171), channel_id=1, source_target_pairs={{0,1},{1,2},{2,3},{4,5},{5,6},{6,7},{8,9},{9,10},{10,11},{12,13},{... | collective-permute-start | bytes 776 | tf_op jit(solution)/shard_map/while/body/eval_jaxpr/ppermute | solution.py:16
  107.2 14.4 %all-to-all-start = ((bf16[64,4,128]{2,1,0:T(4,128)(2,1)}), bf16[64,4,128]{2,1,0:T(4,128)(2,1)S(1)}, u32[]{:S(2)}, u32[]{:S(2)}) async-start(bf16[64,4,128]{2,1,0:T(4,128)(2,1)} %broadcast_select_fusion.2), calls=%async_computation | async-start | bytes 131072 | tf_op jit(solution)/shard_map/while/body/eval_jaxpr/all_to_all | solution.py:65
  121.7 6.3 %collective-permute-start = (bf16[128,1]{1,0:T(8,128)(2,1)S(1)}, bf16[128,1]{1,0:T(8,128)(2,1)S(1)}, u32[]{:S(2)}, u32[]{:S(2)}) collective-permute-start(bf16[128,1]{1,0:T(8,128)(2,1)S(1)} %get-tuple-element.170), channel_id=1, source_target_pairs={{1,0},{2,1},{3,2},{5,4},{6,5},{7,6},{9,8},{10,9},{11,10},{13,12},{... | collective-permute-start | bytes 776 | tf_op jit(solution)/shard_map/while/body/eval_jaxpr/ppermute | solution.py:19
  123.0 6.4 %collective-permute-start.1 = (bf16[128,1]{1,0:T(8,128)(2,1)S(1)}, bf16[128,1]{1,0:T(8,128)(2,1)S(1)}, u32[]{:S(2)}, u32[]{:S(2)}) collective-permute-start(bf16[128,1]{1,0:T(8,128)(2,1)S(1)} %get-tuple-element.171), channel_id=1, source_target_pairs={{0,1},{1,2},{2,3},{4,5},{5,6},{6,7},{8,9},{9,10},{10,11},{12,13},{... | collective-permute-start | bytes 776 | tf_op jit(solution)/shard_map/while/body/eval_jaxpr/ppermute | solution.py:16
  132.4 14.4 %all-to-all-start = ((bf16[64,4,128]{2,1,0:T(4,128)(2,1)}), bf16[64,4,128]{2,1,0:T(4,128)(2,1)S(1)}, u32[]{:S(2)}, u32[]{:S(2)}) async-start(bf16[64,4,128]{2,1,0:T(4,128)(2,1)} %broadcast_select_fusion.2), calls=%async_computation | async-start | bytes 131072 | tf_op jit(solution)/shard_map/while/body/eval_jaxpr/all_to_all | solution.py:65
  146.9 6.3 %collective-permute-start = (bf16[128,1]{1,0:T(8,128)(2,1)S(1)}, bf16[128,1]{1,0:T(8,128)(2,1)S(1)}, u32[]{:S(2)}, u32[]{:S(2)}) collective-permute-start(bf16[128,1]{1,0:T(8,128)(2,1)S(1)} %get-tuple-element.170), channel_id=1, source_target_pairs={{1,0},{2,1},{3,2},{5,4},{6,5},{7,6},{9,8},{10,9},{11,10},{13,12},{... | collective-permute-start | bytes 776 | tf_op jit(solution)/shard_map/while/body/eval_jaxpr/ppermute | solution.py:19
  148.2 6.4 %collective-permute-start.1 = (bf16[128,1]{1,0:T(8,128)(2,1)S(1)}, bf16[128,1]{1,0:T(8,128)(2,1)S(1)}, u32[]{:S(2)}, u32[]{:S(2)}) collective-permute-start(bf16[128,1]{1,0:T(8,128)(2,1)S(1)} %get-tuple-element.171), channel_id=1, source_target_pairs={{0,1},{1,2},{2,3},{4,5},{5,6},{6,7},{8,9},{9,10},{10,11},{12,13},{... | collective-permute-start | bytes 776 | tf_op jit(solution)/shard_map/while/body/eval_jaxpr/ppermute | solution.py:16
  157.7 14.4 %all-to-all-start = ((bf16[64,4,128]{2,1,0:T(4,128)(2,1)}), bf16[64,4,128]{2,1,0:T(4,128)(2,1)S(1)}, u32[]{:S(2)}, u32[]{:S(2)}) async-start(bf16[64,4,128]{2,1,0:T(4,128)(2,1)} %broadcast_select_fusion.2), calls=%async_computation | async-start | bytes 131072 | tf_op jit(solution)/shard_map/while/body/eval_jaxpr/all_to_all | solution.py:65
  172.2 6.3 %collective-permute-start = (bf16[128,1]{1,0:T(8,128)(2,1)S(1)}, bf16[128,1]{1,0:T(8,128)(2,1)S(1)}, u32[]{:S(2)}, u32[]{:S(2)}) collective-permute-start(bf16[128,1]{1,0:T(8,128)(2,1)S(1)} %get-tuple-element.170), channel_id=1, source_target_pairs={{1,0},{2,1},{3,2},{5,4},{6,5},{7,6},{9,8},{10,9},{11,10},{13,12},{... | collective-permute-start | bytes 776 | tf_op jit(solution)/shard_map/while/body/eval_jaxpr/ppermute | solution.py:19
  173.5 6.4 %collective-permute-start.1 = (bf16[128,1]{1,0:T(8,128)(2,1)S(1)}, bf16[128,1]{1,0:T(8,128)(2,1)S(1)}, u32[]{:S(2)}, u32[]{:S(2)}) collective-permute-start(bf16[128,1]{1,0:T(8,128)(2,1)S(1)} %get-tuple-element.171), channel_id=1, source_target_pairs={{0,1},{1,2},{2,3},{4,5},{5,6},{6,7},{8,9},{9,10},{10,11},{12,13},{... | collective-permute-start | bytes 776 | tf_op jit(solution)/shard_map/while/body/eval_jaxpr/ppermute | solution.py:16
  182.9 14.4 %all-to-all-start = ((bf16[64,4,128]{2,1,0:T(4,128)(2,1)}), bf16[64,4,128]{2,1,0:T(4,128)(2,1)S(1)}, u32[]{:S(2)}, u32[]{:S(2)}) async-start(bf16[64,4,128]{2,1,0:T(4,128)(2,1)} %broadcast_select_fusion.2), calls=%async_computation | async-start | bytes 131072 | tf_op jit(solution)/shard_map/while/body/eval_jaxpr/all_to_all | solution.py:65
  197.5 6.3 %collective-permute-start = (bf16[128,1]{1,0:T(8,128)(2,1)S(1)}, bf16[128,1]{1,0:T(8,128)(2,1)S(1)}, u32[]{:S(2)}, u32[]{:S(2)}) collective-permute-start(bf16[128,1]{1,0:T(8,128)(2,1)S(1)} %get-tuple-element.170), channel_id=1, source_target_pairs={{1,0},{2,1},{3,2},{5,4},{6,5},{7,6},{9,8},{10,9},{11,10},{13,12},{... | collective-permute-start | bytes 776 | tf_op jit(solution)/shard_map/while/body/eval_jaxpr/ppermute | solution.py:19
  198.7 6.4 %collective-permute-start.1 = (bf16[128,1]{1,0:T(8,128)(2,1)S(1)}, bf16[128,1]{1,0:T(8,128)(2,1)S(1)}, u32[]{:S(2)}, u32[]{:S(2)}) collective-permute-start(bf16[128,1]{1,0:T(8,128)(2,1)S(1)} %get-tuple-element.171), channel_id=1, source_target_pairs={{0,1},{1,2},{2,3},{4,5},{5,6},{6,7},{8,9},{9,10},{10,11},{12,13},{... | collective-permute-start | bytes 776 | tf_op jit(solution)/shard_map/while/body/eval_jaxpr/ppermute | solution.py:16
  208.2 14.4 %all-to-all-start = ((bf16[64,4,128]{2,1,0:T(4,128)(2,1)}), bf16[64,4,128]{2,1,0:T(4,128)(2,1)S(1)}, u32[]{:S(2)}, u32[]{:S(2)}) async-start(bf16[64,4,128]{2,1,0:T(4,128)(2,1)} %broadcast_select_fusion.2), calls=%async_computation | async-start | bytes 131072 | tf_op jit(solution)/shard_map/while/body/eval_jaxpr/all_to_all | solution.py:65
  222.6 248.6 %copy-start = (f32[128,128]{1,0:T(8,128)}, f32[128,128]{1,0:T(8,128)S(1)}, u32[]{:S(2)}) copy-start(f32[128,128]{1,0:T(8,128)S(1)} %get-tuple-element.81) | copy-start | bytes 196612
  222.6 6.0 %copy-start.1 = (s32[1,128,2]{1,2,0:T(2,128)S(1)}, s32[1,128,2]{1,2,0:T(2,128)}, u32[]{:S(2)}) copy-start(s32[1,128,2]{1,2,0:T(2,128)} %param.18) | copy-start | bytes 3076
Sparse Core Ops, SparseCore 0:
  230.2 239.5 all-reduce.2
where the time goes:
time: 480 us; the launch traced here: 478 us
  waiting for transfers between devices  322 us (67%)
  starting transfers between devices  99.5 us (21%)
  matrix products  15.6 us (3%)
  local copies, waits for them, and re-layouts  14.6 us (3%)
  between operations  14.1 us (3%)
  other arithmetic  11.6 us (2%)
    psum x1, waiting for transfers between devices, on_device(): summed = lax.psum(partial_sum, ('tile', 'sec'))  240 us
    all_to_all x8, waiting for transfers between devices, advance_send(): lax.all_to_all(outgoing, 'tile', split_axis=0, concat_axis=0, tiled=True)  70.7 us
    all_to_all x8, starting transfers between devices, advance_send(): lax.all_to_all(outgoing, 'tile', split_axis=0, concat_axis=0, tiled=True)  50.7 us
    ppermute x8, starting transfers between devices, padded_2(): lax.ppermute(lax.slice_in_dim(block, block.shape[dim] - width, None, axis...  38.5 us
    ppermute x8, waiting for transfers between devices, padded_2(): lax.ppermute(lax.slice_in_dim(block, block.shape[dim] - width, None, axis...  11.2 us
    ppermute x8, starting transfers between devices, padded_2(): lax.ppermute(lax.slice_in_dim(block, 0, width, axis=dim), axis, backward)  10.3 us
    dot_general x8, matrix products, cable_update(): jnp.einsum('ci,ji->cj', right_side, inv_cable, precision=lax.Precision.HI...  10.2 us
  transfers between devices with their start and end apart: 25, of which 17 were waited for; matrix products, arithmetic and copies ran while one was open for 0% of the time, Pallas kernels for 0%

commit v1 on v0

--- a/solution.py
+++ b/solution.py
@@ -85,7 +85,9 @@
     )
     partial_sum = jnp.einsum("tskc,skq->tqc", tile_sums, select, precision=lax.Precision.HIGHEST)
     partial_sum = partial_sum.reshape(step_count, tile_total * contact_width)
-    summed = lax.psum(partial_sum, ("tile", "sec"))
+    summed = partial_sum
+    for no in ("tile", "sec"):
+        summed = lax.psum(summed, no)
     share_width = summed.shape[1] // (tile_count * section_count)
     position = lax.axis_index("tile") * section_count + lax.axis_index("sec")
     probe_share = lax.dynamic_slice_in_dim(summed, position * share_width, share_width, 1)

time: 480 us -> 457 us (0.952)
  waiting for transfers between devices: 322 us -> 299 us
    psum x1 -> x2, waiting for transfers between devices: 240 us -> 217 us  [on_device(): summed = lax.psum(summed, no)]
  transfers between devices with their start and end apart: 25 -> 26, of which waited for: 17 -> 18; matrix products, arithmetic and copies ran while one was open for 0% -> 0% of each run, Pallas kernels for 0% -> 0%
where the time goes in v1:
time: 457 us; the launch traced here: 455 us
  waiting for transfers between devices  299 us (65%)
  starting transfers between devices  99.5 us (22%)
  matrix products  15.6 us (3%)
  local copies, waits for them, and re-layouts  14.6 us (3%)
  between operations  14.1 us (3%)
  other arithmetic  11.6 us (3%)
    psum x2, waiting for transfers between devices, on_device(): summed = lax.psum(summed, no)  217 us
    all_to_all x8, waiting for transfers between devices, advance_send(): lax.all_to_all(outgoing, 'tile', split_axis=0, concat_axis=0, tiled=True)  70.7 us
    all_to_all x8, starting transfers between devices, advance_send(): lax.all_to_all(outgoing, 'tile', split_axis=0, concat_axis=0, tiled=True)  50.6 us
    ppermute x8, starting transfers between devices, padded_2(): lax.ppermute(lax.slice_in_dim(block, block.shape[dim] - width, None, axis...  38.5 us
    ppermute x8, waiting for transfers between devices, padded_2(): lax.ppermute(lax.slice_in_dim(block, block.shape[dim] - width, None, axis...  11.2 us
    ppermute x8, starting transfers between devices, padded_2(): lax.ppermute(lax.slice_in_dim(block, 0, width, axis=dim), axis, backward)  10.3 us
    dot_general x8, matrix products, cable_update(): jnp.einsum('ci,ji->cj', right_side, inv_cable, precision=lax.Precision.HI...  10.2 us
  transfers between devices with their start and end apart: 26, of which 18 were waited for; matrix products, arithmetic and copies ran while one was open for 0% of the time, Pallas kernels for 0%

profile of v1, /device:TPU:8, one launch (start us, length us, event | category | flops | bytes accessed | tf_op | source)
XLA Modules:
  0.0 455.3 jit_solution(10041813562831894835)
XLA Ops:
  14.3 208.3 %while.13 = (s32[]{:T(128)}, f32[128,128]{1,0:T(8,128)S(1)}, bf16[8,64,4,128]{3,2,1,0:T(4,128)(2,1)S(1)}, f32[128,128]{1,0:T(8,128)}, bf16[8,128,128]{2,1,0:T(8,...) while((s32[]{:T(128)}, f32[128,128]{1,0:T(8,128)S(1)}, ...), condition=%wide.region_4.5_spmd, body=%wide.region_3.4_spmd.sunk | while | flops 25629952 | bytes 1626603 | solution.py:68
  15.7 4.5 collective-permute-start.1
  20.4 1.4 collective-permute-done.1
  24.8 12.1 %all-to-all-start = ((bf16[64,4,128]{2,1,0:T(4,128)(2,1)}), bf16[64,4,128]{2,1,0:T(4,128)(2,1)S(1)}, u32[]{:S(2)}, u32[]{:S(2)}) async-start(bf16[64,4,128]{2,1,0:T(4,128)(2,1)} %broadcast_select_fusion.2), calls=%async_computation | async-start | bytes 131072 | tf_op jit(solution)/shard_map/while/body/eval_jaxpr/all_to_all | solution.py:65
  36.9 8.8 %all-to-all-done = bf16[64,4,128]{2,1,0:T(4,128)(2,1)S(1)} async-done(((bf16[64,4,128]{2,1,0:T(4,128)(2,1)}), bf16[64,4,128]{2,1,0:T(4,128)(2,1)S(1)}, u32[]{:S(2)}, u32[]{:S(2)}) %all-to-all-start) | async-done | bytes 65568 | tf_op jit(solution)/shard_map/while/body/eval_jaxpr/all_to_all | solution.py:65
  47.2 4.9 %collective-permute-start.1 = (bf16[128,1]{1,0:T(8,128)(2,1)S(1)}, bf16[128,1]{1,0:T(8,128)(2,1)S(1)}, u32[]{:S(2)}, u32[]{:S(2)}) collective-permute-start(bf16[128,1]{1,0:T(8,128)(2,1)S(1)} %get-tuple-element.171), channel_id=1, source_target_pairs={{0,1},{1,2},{2,3},{4,5},{5,6},{6,7},{8,9},{9,10},{10,11},{12,13},{... | collective-permute-start | bytes 776 | tf_op jit(solution)/shard_map/while/body/eval_jaxpr/ppermute | solution.py:16
  52.2 1.4 collective-permute-done.1
  56.7 5.5 %all-to-all-start = ((bf16[64,4,128]{2,1,0:T(4,128)(2,1)}), bf16[64,4,128]{2,1,0:T(4,128)(2,1)S(1)}, u32[]{:S(2)}, u32[]{:S(2)}) async-start(bf16[64,4,128]{2,1,0:T(4,128)(2,1)} %broadcast_select_fusion.2), calls=%async_computation | async-start | bytes 131072 | tf_op jit(solution)/shard_map/while/body/eval_jaxpr/all_to_all | solution.py:65
  62.2 8.8 %all-to-all-done = bf16[64,4,128]{2,1,0:T(4,128)(2,1)S(1)} async-done(((bf16[64,4,128]{2,1,0:T(4,128)(2,1)}), bf16[64,4,128]{2,1,0:T(4,128)(2,1)S(1)}, u32[]{:S(2)}, u32[]{:S(2)}) %all-to-all-start) | async-done | bytes 65568 | tf_op jit(solution)/shard_map/while/body/eval_jaxpr/all_to_all | solution.py:65
  72.5 4.9 %collective-permute-start.1 = (bf16[128,1]{1,0:T(8,128)(2,1)S(1)}, bf16[128,1]{1,0:T(8,128)(2,1)S(1)}, u32[]{:S(2)}, u32[]{:S(2)}) collective-permute-start(bf16[128,1]{1,0:T(8,128)(2,1)S(1)} %get-tuple-element.171), channel_id=1, source_target_pairs={{0,1},{1,2},{2,3},{4,5},{5,6},{6,7},{8,9},{9,10},{10,11},{12,13},{... | collective-permute-start | bytes 776 | tf_op jit(solution)/shard_map/while/body/eval_jaxpr/ppermute | solution.py:16
  77.5 1.4 collective-permute-done.1
  81.9 5.5 %all-to-all-start = ((bf16[64,4,128]{2,1,0:T(4,128)(2,1)}), bf16[64,4,128]{2,1,0:T(4,128)(2,1)S(1)}, u32[]{:S(2)}, u32[]{:S(2)}) async-start(bf16[64,4,128]{2,1,0:T(4,128)(2,1)} %broadcast_select_fusion.2), calls=%async_computation | async-start | bytes 131072 | tf_op jit(solution)/shard_map/while/body/eval_jaxpr/all_to_all | solution.py:65
  87.4 8.8 %all-to-all-done = bf16[64,4,128]{2,1,0:T(4,128)(2,1)S(1)} async-done(((bf16[64,4,128]{2,1,0:T(4,128)(2,1)}), bf16[64,4,128]{2,1,0:T(4,128)(2,1)S(1)}, u32[]{:S(2)}, u32[]{:S(2)}) %all-to-all-start) | async-done | bytes 65568 | tf_op jit(solution)/shard_map/while/body/eval_jaxpr/all_to_all | solution.py:65
  97.7 4.9 %collective-permute-start.1 = (bf16[128,1]{1,0:T(8,128)(2,1)S(1)}, bf16[128,1]{1,0:T(8,128)(2,1)S(1)}, u32[]{:S(2)}, u32[]{:S(2)}) collective-permute-start(bf16[128,1]{1,0:T(8,128)(2,1)S(1)} %get-tuple-element.171), channel_id=1, source_target_pairs={{0,1},{1,2},{2,3},{4,5},{5,6},{6,7},{8,9},{9,10},{10,11},{12,13},{... | collective-permute-start | bytes 776 | tf_op jit(solution)/shard_map/while/body/eval_jaxpr/ppermute | solution.py:16
  107.2 5.5 %all-to-all-start = ((bf16[64,4,128]{2,1,0:T(4,128)(2,1)}), bf16[64,4,128]{2,1,0:T(4,128)(2,1)S(1)}, u32[]{:S(2)}, u32[]{:S(2)}) async-start(bf16[64,4,128]{2,1,0:T(4,128)(2,1)} %broadcast_select_fusion.2), calls=%async_computation | async-start | bytes 131072 | tf_op jit(solution)/shard_map/while/body/eval_jaxpr/all_to_all | solution.py:65
  112.7 8.8 %all-to-all-done = bf16[64,4,128]{2,1,0:T(4,128)(2,1)S(1)} async-done(((bf16[64,4,128]{2,1,0:T(4,128)(2,1)}), bf16[64,4,128]{2,1,0:T(4,128)(2,1)S(1)}, u32[]{:S(2)}, u32[]{:S(2)}) %all-to-all-start) | async-done | bytes 65568 | tf_op jit(solution)/shard_map/while/body/eval_jaxpr/all_to_all | solution.py:65
  123.0 4.8 %collective-permute-start.1 = (bf16[128,1]{1,0:T(8,128)(2,1)S(1)}, bf16[128,1]{1,0:T(8,128)(2,1)S(1)}, u32[]{:S(2)}, u32[]{:S(2)}) collective-permute-start(bf16[128,1]{1,0:T(8,128)(2,1)S(1)} %get-tuple-element.171), channel_id=1, source_target_pairs={{0,1},{1,2},{2,3},{4,5},{5,6},{6,7},{8,9},{9,10},{10,11},{12,13},{... | collective-permute-start | bytes 776 | tf_op jit(solution)/shard_map/while/body/eval_jaxpr/ppermute | solution.py:16
  132.4 5.5 %all-to-all-start = ((bf16[64,4,128]{2,1,0:T(4,128)(2,1)}), bf16[64,4,128]{2,1,0:T(4,128)(2,1)S(1)}, u32[]{:S(2)}, u32[]{:S(2)}) async-start(bf16[64,4,128]{2,1,0:T(4,128)(2,1)} %broadcast_select_fusion.2), calls=%async_computation | async-start | bytes 131072 | tf_op jit(solution)/shard_map/while/body/eval_jaxpr/all_to_all | solution.py:65
  137.9 8.8 %all-to-all-done = bf16[64,4,128]{2,1,0:T(4,128)(2,1)S(1)} async-done(((bf16[64,4,128]{2,1,0:T(4,128)(2,1)}), bf16[64,4,128]{2,1,0:T(4,128)(2,1)S(1)}, u32[]{:S(2)}, u32[]{:S(2)}) %all-to-all-start) | async-done | bytes 65568 | tf_op jit(solution)/shard_map/while/body/eval_jaxpr/all_to_all | solution.py:65
  148.2 4.9 %collective-permute-start.1 = (bf16[128,1]{1,0:T(8,128)(2,1)S(1)}, bf16[128,1]{1,0:T(8,128)(2,1)S(1)}, u32[]{:S(2)}, u32[]{:S(2)}) collective-permute-start(bf16[128,1]{1,0:T(8,128)(2,1)S(1)} %get-tuple-element.171), channel_id=1, source_target_pairs={{0,1},{1,2},{2,3},{4,5},{5,6},{6,7},{8,9},{9,10},{10,11},{12,13},{... | collective-permute-start | bytes 776 | tf_op jit(solution)/shard_map/while/body/eval_jaxpr/ppermute | solution.py:16
  157.7 5.5 %all-to-all-start = ((bf16[64,4,128]{2,1,0:T(4,128)(2,1)}), bf16[64,4,128]{2,1,0:T(4,128)(2,1)S(1)}, u32[]{:S(2)}, u32[]{:S(2)}) async-start(bf16[64,4,128]{2,1,0:T(4,128)(2,1)} %broadcast_select_fusion.2), calls=%async_computation | async-start | bytes 131072 | tf_op jit(solution)/shard_map/while/body/eval_jaxpr/all_to_all | solution.py:65
  163.2 8.8 %all-to-all-done = bf16[64,4,128]{2,1,0:T(4,128)(2,1)S(1)} async-done(((bf16[64,4,128]{2,1,0:T(4,128)(2,1)}), bf16[64,4,128]{2,1,0:T(4,128)(2,1)S(1)}, u32[]{:S(2)}, u32[]{:S(2)}) %all-to-all-start) | async-done | bytes 65568 | tf_op jit(solution)/shard_map/while/body/eval_jaxpr/all_to_all | solution.py:65
  173.5 4.9 %collective-permute-start.1 = (bf16[128,1]{1,0:T(8,128)(2,1)S(1)}, bf16[128,1]{1,0:T(8,128)(2,1)S(1)}, u32[]{:S(2)}, u32[]{:S(2)}) collective-permute-start(bf16[128,1]{1,0:T(8,128)(2,1)S(1)} %get-tuple-element.171), channel_id=1, source_target_pairs={{0,1},{1,2},{2,3},{4,5},{5,6},{6,7},{8,9},{9,10},{10,11},{12,13},{... | collective-permute-start | bytes 776 | tf_op jit(solution)/shard_map/while/body/eval_jaxpr/ppermute | solution.py:16
  182.9 5.5 %all-to-all-start = ((bf16[64,4,128]{2,1,0:T(4,128)(2,1)}), bf16[64,4,128]{2,1,0:T(4,128)(2,1)S(1)}, u32[]{:S(2)}, u32[]{:S(2)}) async-start(bf16[64,4,128]{2,1,0:T(4,128)(2,1)} %broadcast_select_fusion.2), calls=%async_computation | async-start | bytes 131072 | tf_op jit(solution)/shard_map/while/body/eval_jaxpr/all_to_all | solution.py:65
  188.4 8.8 %all-to-all-done = bf16[64,4,128]{2,1,0:T(4,128)(2,1)S(1)} async-done(((bf16[64,4,128]{2,1,0:T(4,128)(2,1)}), bf16[64,4,128]{2,1,0:T(4,128)(2,1)S(1)}, u32[]{:S(2)}, u32[]{:S(2)}) %all-to-all-start) | async-done | bytes 65568 | tf_op jit(solution)/shard_map/while/body/eval_jaxpr/all_to_all | solution.py:65
  198.7 4.8 %collective-permute-start.1 = (bf16[128,1]{1,0:T(8,128)(2,1)S(1)}, bf16[128,1]{1,0:T(8,128)(2,1)S(1)}, u32[]{:S(2)}, u32[]{:S(2)}) collective-permute-start(bf16[128,1]{1,0:T(8,128)(2,1)S(1)} %get-tuple-element.171), channel_id=1, source_target_pairs={{0,1},{1,2},{2,3},{4,5},{5,6},{6,7},{8,9},{9,10},{10,11},{12,13},{... | collective-permute-start | bytes 776 | tf_op jit(solution)/shard_map/while/body/eval_jaxpr/ppermute | solution.py:16
  203.8 1.4 collective-permute-done.1
  208.2 5.5 %all-to-all-start = ((bf16[64,4,128]{2,1,0:T(4,128)(2,1)}), bf16[64,4,128]{2,1,0:T(4,128)(2,1)S(1)}, u32[]{:S(2)}, u32[]{:S(2)}) async-start(bf16[64,4,128]{2,1,0:T(4,128)(2,1)} %broadcast_select_fusion.2), calls=%async_computation | async-start | bytes 131072 | tf_op jit(solution)/shard_map/while/body/eval_jaxpr/all_to_all | solution.py:65
  213.7 8.8 %all-to-all-done = bf16[64,4,128]{2,1,0:T(4,128)(2,1)S(1)} async-done(((bf16[64,4,128]{2,1,0:T(4,128)(2,1)}), bf16[64,4,128]{2,1,0:T(4,128)(2,1)S(1)}, u32[]{:S(2)}, u32[]{:S(2)}) %all-to-all-start) | async-done | bytes 65568 | tf_op jit(solution)/shard_map/while/body/eval_jaxpr/all_to_all | solution.py:65
  223.9 4.6 %fusion.28 = f32[8,128,2,128]{3,0,2,1:T(8,128)S(1)} fusion(bf16[1,128,2,128,128]{4,3,2,1,0:T(8,128)(2,1)} %param.19, bf16[128,8,128]{2,1,0:T(8,128)(2,1)S(1)} %gather_fusion.1, pred[128]{0:T(512)(128)(4,1)S(1)} %compare_and_fusion.1), kind=kOutput, calls=%fused_computation.41 | convolution fusion | flops 67239936 | bytes 9699456 | tf_op jit(solution)/shard_map/tsi,skic->tskc/dot_general | solution.py:82
  230.1 169.8 %all-reduce.4.cloned.1.call-done = f32[8,4096]{1,0:T(8,128)} async-done(((f32[8,4096]{1,0:T(8,128)}), f32[8,4096]{1,0:T(8,128)}) %all-reduce.4.cloned.1.call-update) | async-done | bytes 131088 | tf_op jit(solution)/shard_map/psum | solution.py:90
  400.0 47.1 %all-reduce.6.cloned.1.call-done = f32[8,4096]{1,0:T(8,128)} async-done(((f32[8,4096]{1,0:T(8,128)}), f32[8,4096]{1,0:T(8,128)}) %all-reduce.6.cloned.1.call-update) | async-done | bytes 131088 | tf_op jit(solution)/shard_map/psum | solution.py:90
  (163 shorter events, 53.2 us)
Async XLA Ops:
  7.2 392.8 %all-reduce.4.cloned.1.call-start = ((), (), s32[]{:S(2)}) async-start(), calls=%async_computation.1 | async-start | bytes 262144 | tf_op jit(solution)/shard_map/psum | solution.py:90
  14.4 6.0 %collective-permute-start = (bf16[128,1]{1,0:T(8,128)(2,1)S(1)}, bf16[128,1]{1,0:T(8,128)(2,1)S(1)}, u32[]{:S(2)}, u32[]{:S(2)}) collective-permute-start(bf16[128,1]{1,0:T(8,128)(2,1)S(1)} %get-tuple-element.170), channel_id=1, source_target_pairs={{1,0},{2,1},{3,2},{5,4},{6,5},{7,6},{9,8},{10,9},{11,10},{13,12},{... | collective-permute-start | bytes 776 | tf_op jit(solution)/shard_map/while/body/eval_jaxpr/ppermute | solution.py:19
  15.7 6.1 %collective-permute-start.1 = (bf16[128,1]{1,0:T(8,128)(2,1)S(1)}, bf16[128,1]{1,0:T(8,128)(2,1)S(1)}, u32[]{:S(2)}, u32[]{:S(2)}) collective-permute-start(bf16[128,1]{1,0:T(8,128)(2,1)S(1)} %get-tuple-element.171), channel_id=1, source_target_pairs={{0,1},{1,2},{2,3},{4,5},{5,6},{6,7},{8,9},{9,10},{10,11},{12,13},{... | collective-permute-start | bytes 776 | tf_op jit(solution)/shard_map/while/body/eval_jaxpr/ppermute | solution.py:16
  24.8 20.9 %all-to-all-start = ((bf16[64,4,128]{2,1,0:T(4,128)(2,1)}), bf16[64,4,128]{2,1,0:T(4,128)(2,1)S(1)}, u32[]{:S(2)}, u32[]{:S(2)}) async-start(bf16[64,4,128]{2,1,0:T(4,128)(2,1)} %broadcast_select_fusion.2), calls=%async_computation | async-start | bytes 131072 | tf_op jit(solution)/shard_map/while/body/eval_jaxpr/all_to_all | solution.py:65
  45.9 6.3 %collective-permute-start = (bf16[128,1]{1,0:T(8,128)(2,1)S(1)}, bf16[128,1]{1,0:T(8,128)(2,1)S(1)}, u32[]{:S(2)}, u32[]{:S(2)}) collective-permute-start(bf16[128,1]{1,0:T(8,128)(2,1)S(1)} %get-tuple-element.170), channel_id=1, source_target_pairs={{1,0},{2,1},{3,2},{5,4},{6,5},{7,6},{9,8},{10,9},{11,10},{13,12},{... | collective-permute-start | bytes 776 | tf_op jit(solution)/shard_map/while/body/eval_jaxpr/ppermute | solution.py:19
  47.2 6.4 %collective-permute-start.1 = (bf16[128,1]{1,0:T(8,128)(2,1)S(1)}, bf16[128,1]{1,0:T(8,128)(2,1)S(1)}, u32[]{:S(2)}, u32[]{:S(2)}) collective-permute-start(bf16[128,1]{1,0:T(8,128)(2,1)S(1)} %get-tuple-element.171), channel_id=1, source_target_pairs={{0,1},{1,2},{2,3},{4,5},{5,6},{6,7},{8,9},{9,10},{10,11},{12,13},{... | collective-permute-start | bytes 776 | tf_op jit(solution)/shard_map/while/body/eval_jaxpr/ppermute | solution.py:16
  56.7 14.4 %all-to-all-start = ((bf16[64,4,128]{2,1,0:T(4,128)(2,1)}), bf16[64,4,128]{2,1,0:T(4,128)(2,1)S(1)}, u32[]{:S(2)}, u32[]{:S(2)}) async-start(bf16[64,4,128]{2,1,0:T(4,128)(2,1)} %broadcast_select_fusion.2), calls=%async_computation | async-start | bytes 131072 | tf_op jit(solution)/shard_map/while/body/eval_jaxpr/all_to_all | solution.py:65
  71.2 6.3 %collective-permute-start = (bf16[128,1]{1,0:T(8,128)(2,1)S(1)}, bf16[128,1]{1,0:T(8,128)(2,1)S(1)}, u32[]{:S(2)}, u32[]{:S(2)}) collective-permute-start(bf16[128,1]{1,0:T(8,128)(2,1)S(1)} %get-tuple-element.170), channel_id=1, source_target_pairs={{1,0},{2,1},{3,2},{5,4},{6,5},{7,6},{9,8},{10,9},{11,10},{13,12},{... | collective-permute-start | bytes 776 | tf_op jit(solution)/shard_map/while/body/eval_jaxpr/ppermute | solution.py:19
  72.5 6.4 %collective-permute-start.1 = (bf16[128,1]{1,0:T(8,128)(2,1)S(1)}, bf16[128,1]{1,0:T(8,128)(2,1)S(1)}, u32[]{:S(2)}, u32[]{:S(2)}) collective-permute-start(bf16[128,1]{1,0:T(8,128)(2,1)S(1)} %get-tuple-element.171), channel_id=1, source_target_pairs={{0,1},{1,2},{2,3},{4,5},{5,6},{6,7},{8,9},{9,10},{10,11},{12,13},{... | collective-permute-start | bytes 776 | tf_op jit(solution)/shard_map/while/body/eval_jaxpr/ppermute | solution.py:16
  81.9 14.3 %all-to-all-start = ((bf16[64,4,128]{2,1,0:T(4,128)(2,1)}), bf16[64,4,128]{2,1,0:T(4,128)(2,1)S(1)}, u32[]{:S(2)}, u32[]{:S(2)}) async-start(bf16[64,4,128]{2,1,0:T(4,128)(2,1)} %broadcast_select_fusion.2), calls=%async_computation | async-start | bytes 131072 | tf_op jit(solution)/shard_map/while/body/eval_jaxpr/all_to_all | solution.py:65
  96.4 6.3 %collective-permute-start = (bf16[128,1]{1,0:T(8,128)(2,1)S(1)}, bf16[128,1]{1,0:T(8,128)(2,1)S(1)}, u32[]{:S(2)}, u32[]{:S(2)}) collective-permute-start(bf16[128,1]{1,0:T(8,128)(2,1)S(1)} %get-tuple-element.170), channel_id=1, source_target_pairs={{1,0},{2,1},{3,2},{5,4},{6,5},{7,6},{9,8},{10,9},{11,10},{13,12},{... | collective-permute-start | bytes 776 | tf_op jit(solution)/shard_map/while/body/eval_jaxpr/ppermute | solution.py:19
  97.7 6.4 %collective-permute-start.1 = (bf16[128,1]{1,0:T(8,128)(2,1)S(1)}, bf16[128,1]{1,0:T(8,128)(2,1)S(1)}, u32[]{:S(2)}, u32[]{:S(2)}) collective-permute-start(bf16[128,1]{1,0:T(8,128)(2,1)S(1)} %get-tuple-element.171), channel_id=1, source_target_pairs={{0,1},{1,2},{2,3},{4,5},{5,6},{6,7},{8,9},{9,10},{10,11},{12,13},{... | collective-permute-start | bytes 776 | tf_op jit(solution)/shard_map/while/body/eval_jaxpr/ppermute | solution.py:16
  107.2 14.3 %all-to-all-start = ((bf16[64,4,128]{2,1,0:T(4,128)(2,1)}), bf16[64,4,128]{2,1,0:T(4,128)(2,1)S(1)}, u32[]{:S(2)}, u32[]{:S(2)}) async-start(bf16[64,4,128]{2,1,0:T(4,128)(2,1)} %broadcast_select_fusion.2), calls=%async_computation | async-start | bytes 131072 | tf_op jit(solution)/shard_map/while/body/eval_jaxpr/all_to_all | solution.py:65
  121.7 6.3 %collective-permute-start = (bf16[128,1]{1,0:T(8,128)(2,1)S(1)}, bf16[128,1]{1,0:T(8,128)(2,1)S(1)}, u32[]{:S(2)}, u32[]{:S(2)}) collective-permute-start(bf16[128,1]{1,0:T(8,128)(2,1)S(1)} %get-tuple-element.170), channel_id=1, source_target_pairs={{1,0},{2,1},{3,2},{5,4},{6,5},{7,6},{9,8},{10,9},{11,10},{13,12},{... | collective-permute-start | bytes 776 | tf_op jit(solution)/shard_map/while/body/eval_jaxpr/ppermute | solution.py:19
  123.0 6.4 %collective-permute-start.1 = (bf16[128,1]{1,0:T(8,128)(2,1)S(1)}, bf16[128,1]{1,0:T(8,128)(2,1)S(1)}, u32[]{:S(2)}, u32[]{:S(2)}) collective-permute-start(bf16[128,1]{1,0:T(8,128)(2,1)S(1)} %get-tuple-element.171), channel_id=1, source_target_pairs={{0,1},{1,2},{2,3},{4,5},{5,6},{6,7},{8,9},{9,10},{10,11},{12,13},{... | collective-permute-start | bytes 776 | tf_op jit(solution)/shard_map/while/body/eval_jaxpr/ppermute | solution.py:16
  132.4 14.4 %all-to-all-start = ((bf16[64,4,128]{2,1,0:T(4,128)(2,1)}), bf16[64,4,128]{2,1,0:T(4,128)(2,1)S(1)}, u32[]{:S(2)}, u32[]{:S(2)}) async-start(bf16[64,4,128]{2,1,0:T(4,128)(2,1)} %broadcast_select_fusion.2), calls=%async_computation | async-start | bytes 131072 | tf_op jit(solution)/shard_map/while/body/eval_jaxpr/all_to_all | solution.py:65
  146.9 6.3 %collective-permute-start = (bf16[128,1]{1,0:T(8,128)(2,1)S(1)}, bf16[128,1]{1,0:T(8,128)(2,1)S(1)}, u32[]{:S(2)}, u32[]{:S(2)}) collective-permute-start(bf16[128,1]{1,0:T(8,128)(2,1)S(1)} %get-tuple-element.170), channel_id=1, source_target_pairs={{1,0},{2,1},{3,2},{5,4},{6,5},{7,6},{9,8},{10,9},{11,10},{13,12},{... | collective-permute-start | bytes 776 | tf_op jit(solution)/shard_map/while/body/eval_jaxpr/ppermute | solution.py:19
  148.2 6.4 %collective-permute-start.1 = (bf16[128,1]{1,0:T(8,128)(2,1)S(1)}, bf16[128,1]{1,0:T(8,128)(2,1)S(1)}, u32[]{:S(2)}, u32[]{:S(2)}) collective-permute-start(bf16[128,1]{1,0:T(8,128)(2,1)S(1)} %get-tuple-element.171), channel_id=1, source_target_pairs={{0,1},{1,2},{2,3},{4,5},{5,6},{6,7},{8,9},{9,10},{10,11},{12,13},{... | collective-permute-start | bytes 776 | tf_op jit(solution)/shard_map/while/body/eval_jaxpr/ppermute | solution.py:16
  157.7 14.3 %all-to-all-start = ((bf16[64,4,128]{2,1,0:T(4,128)(2,1)}), bf16[64,4,128]{2,1,0:T(4,128)(2,1)S(1)}, u32[]{:S(2)}, u32[]{:S(2)}) async-start(bf16[64,4,128]{2,1,0:T(4,128)(2,1)} %broadcast_select_fusion.2), calls=%async_computation | async-start | bytes 131072 | tf_op jit(solution)/shard_map/while/body/eval_jaxpr/all_to_all | solution.py:65
  172.2 6.3 %collective-permute-start = (bf16[128,1]{1,0:T(8,128)(2,1)S(1)}, bf16[128,1]{1,0:T(8,128)(2,1)S(1)}, u32[]{:S(2)}, u32[]{:S(2)}) collective-permute-start(bf16[128,1]{1,0:T(8,128)(2,1)S(1)} %get-tuple-element.170), channel_id=1, source_target_pairs={{1,0},{2,1},{3,2},{5,4},{6,5},{7,6},{9,8},{10,9},{11,10},{13,12},{... | collective-permute-start | bytes 776 | tf_op jit(solution)/shard_map/while/body/eval_jaxpr/ppermute | solution.py:19
  173.5 6.4 %collective-permute-start.1 = (bf16[128,1]{1,0:T(8,128)(2,1)S(1)}, bf16[128,1]{1,0:T(8,128)(2,1)S(1)}, u32[]{:S(2)}, u32[]{:S(2)}) collective-permute-start(bf16[128,1]{1,0:T(8,128)(2,1)S(1)} %get-tuple-element.171), channel_id=1, source_target_pairs={{0,1},{1,2},{2,3},{4,5},{5,6},{6,7},{8,9},{9,10},{10,11},{12,13},{... | collective-permute-start | bytes 776 | tf_op jit(solution)/shard_map/while/body/eval_jaxpr/ppermute | solution.py:16
  182.9 14.3 %all-to-all-start = ((bf16[64,4,128]{2,1,0:T(4,128)(2,1)}), bf16[64,4,128]{2,1,0:T(4,128)(2,1)S(1)}, u32[]{:S(2)}, u32[]{:S(2)}) async-start(bf16[64,4,128]{2,1,0:T(4,128)(2,1)} %broadcast_select_fusion.2), calls=%async_computation | async-start | bytes 131072 | tf_op jit(solution)/shard_map/while/body/eval_jaxpr/all_to_all | solution.py:65
  197.4 6.3 %collective-permute-start = (bf16[128,1]{1,0:T(8,128)(2,1)S(1)}, bf16[128,1]{1,0:T(8,128)(2,1)S(1)}, u32[]{:S(2)}, u32[]{:S(2)}) collective-permute-start(bf16[128,1]{1,0:T(8,128)(2,1)S(1)} %get-tuple-element.170), channel_id=1, source_target_pairs={{1,0},{2,1},{3,2},{5,4},{6,5},{7,6},{9,8},{10,9},{11,10},{13,12},{... | collective-permute-start | bytes 776 | tf_op jit(solution)/shard_map/while/body/eval_jaxpr/ppermute | solution.py:19
  198.7 6.4 %collective-permute-start.1 = (bf16[128,1]{1,0:T(8,128)(2,1)S(1)}, bf16[128,1]{1,0:T(8,128)(2,1)S(1)}, u32[]{:S(2)}, u32[]{:S(2)}) collective-permute-start(bf16[128,1]{1,0:T(8,128)(2,1)S(1)} %get-tuple-element.171), channel_id=1, source_target_pairs={{0,1},{1,2},{2,3},{4,5},{5,6},{6,7},{8,9},{9,10},{10,11},{12,13},{... | collective-permute-start | bytes 776 | tf_op jit(solution)/shard_map/while/body/eval_jaxpr/ppermute | solution.py:16
  208.2 14.3 %all-to-all-start = ((bf16[64,4,128]{2,1,0:T(4,128)(2,1)}), bf16[64,4,128]{2,1,0:T(4,128)(2,1)S(1)}, u32[]{:S(2)}, u32[]{:S(2)}) async-start(bf16[64,4,128]{2,1,0:T(4,128)(2,1)} %broadcast_select_fusion.2), calls=%async_computation | async-start | bytes 131072 | tf_op jit(solution)/shard_map/while/body/eval_jaxpr/all_to_all | solution.py:65
  222.6 225.9 %copy-start = (f32[128,128]{1,0:T(8,128)}, f32[128,128]{1,0:T(8,128)S(1)}, u32[]{:S(2)}) copy-start(f32[128,128]{1,0:T(8,128)S(1)} %get-tuple-element.81) | copy-start | bytes 196612
  222.6 6.0 %copy-start.1 = (s32[1,128,2]{1,2,0:T(2,128)S(1)}, s32[1,128,2]{1,2,0:T(2,128)}, u32[]{:S(2)}) copy-start(s32[1,128,2]{1,2,0:T(2,128)} %param.18) | copy-start | bytes 3076
  230.1 217.0 %all-reduce.6.cloned.1.call-start = ((), (), s32[]{:S(2)}) async-start(), calls=%async_computation.2 | async-start | bytes 262144 | tf_op jit(solution)/shard_map/psum | solution.py:90
Sparse Core Ops, SparseCore 0:
  230.2 169.7 all-reduce.3
  402.2 44.8 all-reduce.5
